TPU v7x, 32 devices: a whole 2x2x4 slice. The times are simulated.
32 devices in a mesh: dp: 8 (over z, x), tensor: 4 (over y, core).
Axes of the slice: x: 2, y: 2, z: 4, core: 2. Of those that a mesh axis runs over, the one named last changes fastest.
Arguments:
- tokens: bfloat16 [16384, 768], P('dp'), may hold values from -6 to 6
- seq_lens: int32 [16], P('dp'), may hold values from 512 to 1024, as said below
- block_sizes: int32 [16], P('dp'), may hold values from 128 to 512
- w_query: bfloat16 [768, 768], P('dp', 'tensor'), may hold values from -0.3125 to 0.3125
- b_query: bfloat16 [768], P('tensor'), may hold values from -3 to 3
- w_key: bfloat16 [768, 768], P('dp', 'tensor'), may hold values from -0.21875 to 0.21875
- w_value: bfloat16 [768, 768], P('dp', 'tensor'), may hold values from -0.21875 to 0.21875
- b_value: bfloat16 [768], P('tensor'), may hold values from -3 to 3
- w_out: bfloat16 [768, 768], P('tensor', 'dp'), may hold values from -1.25 to 1.25
- b_out: bfloat16 [768], P('dp'), may hold values from -2 to 2
- gain_one: bfloat16 [768], P('dp'), may hold values from 0.25 to 1.75
- shift_one: bfloat16 [768], P('dp'), may hold values from -2 to 2
- w_up: bfloat16 [768, 3072], P('dp', 'tensor'), may hold values from -0.21875 to 0.21875
- b_up: bfloat16 [3072], P('tensor'), may hold values from -3 to 3
- w_down: bfloat16 [3072, 768], P('tensor', 'dp'), may hold values from -0.109375 to 0.109375
- b_down: bfloat16 [768], P('dp'), may hold values from -2 to 2
- gain_two: bfloat16 [768], P('dp'), may hold values from 0.25 to 1.75
- shift_two: bfloat16 [768], P('dp'), may hold values from -2 to 2
- cotangent: bfloat16 [16384, 768], P('dp'), may hold values from -6 to 6
Outputs:
- output: bfloat16 [16384, 768], P('dp')
- input_grad: float32 [16384, 768], P('dp', 'tensor')
- grad_w_query: float32 [768, 768], P('dp', 'tensor')
- grad_b_query: float32 [768], P('tensor')
- grad_w_key: float32 [768, 768], P('dp', 'tensor')
- grad_w_value: float32 [768, 768], P('dp', 'tensor')
- grad_b_value: float32 [768], P('tensor')
- grad_w_out: float32 [768, 768], P('tensor', 'dp')
- grad_b_out: float32 [768], P('dp')
- grad_gain_one: float32 [768], P('dp')
- grad_shift_one: float32 [768], P('dp')
- grad_w_up: float32 [768, 3072], P('dp', 'tensor')
- grad_b_up: float32 [3072], P('tensor')
- grad_w_down: float32 [3072, 768], P('tensor', 'dp')
- grad_b_down: float32 [768], P('dp')
- grad_gain_two: float32 [768], P('dp')
- grad_shift_two: float32 [768], P('dp')
Inputs may be any that keep to these rules, and one draw needn't show every extreme that they name: seq_lens[s] counts the key positions of sequence s that any query may see; at least one sequence is whole.
All inputs are finite; a program needn't handle non-finite values.
Results may differ from a plain program's by a relative error of at most 0.015.
The roundings to bfloat16 on the way count: a program that leaves them out, or rounds other values in their place, can miss the bound.
Values may be sent and summed in bfloat16 or wider, within the bound.
A program may use at most 192 MiB of HBM per device.

v0:
```python
import jax
import jax.numpy as jnp
from jax import lax
from jax.sharding import PartitionSpec as P

HEAD = 64
norm_epsilon = 1e-12
inv_root_two = 0.7071067811865476
inv_root_tau = 0.3989422804014327
masked_score = -1000000000.0


def matmul(first_operand, second_operand):
    return jnp.dot(first_operand, second_operand, preferred_element_type=jnp.float32)


def contract_rows(first_operand, second_operand):
    return lax.dot_general(
        first_operand, second_operand, (((0,), (0,)), ((), ())), preferred_element_type=jnp.float32
    )


def contract_cols(first_operand, second_operand):
    return lax.dot_general(
        first_operand, second_operand, (((1,), (1,)), ((), ())), preferred_element_type=jnp.float32
    )


def norm_forward(row_values, gain_row, offset_row):
    row_mean = jnp.mean(row_values, axis=-1, keepdims=True)
    centred = row_values - row_mean
    variance = jnp.mean(centred * centred, axis=-1, keepdims=True)
    inv_scale = lax.rsqrt(variance + norm_epsilon)
    normal_rows = centred * inv_scale
    return (normal_rows * gain_row + offset_row, normal_rows, inv_scale)


def norm_backward(upstream, normal_rows, inv_scale, gain_row):
    scaled = upstream * gain_row
    row_grad = inv_scale * (
        scaled
        - jnp.mean(scaled, axis=-1, keepdims=True)
        - normal_rows * jnp.mean(scaled * normal_rows, axis=-1, keepdims=True)
    )
    return (row_grad, jnp.sum(upstream * normal_rows, axis=0), jnp.sum(upstream, axis=0))


def allowed_mask(first_row, row_total, key_total, seq_length, block_size):
    row_pos = first_row + lax.broadcasted_iota(jnp.int32, (row_total, key_total), 0)
    key_pos = lax.broadcasted_iota(jnp.int32, (row_total, key_total), 1)
    return (key_pos // block_size <= row_pos // block_size) & (key_pos < seq_length)


def attend(query_rows, key_rows, value_rows, seq_length, block_size):
    row_total, local_heads, head_size = query_rows.shape
    block_rows = min(512, row_total)
    block_count = row_total // block_rows
    query_blocks = query_rows.reshape(block_count, block_rows, local_heads, head_size)

    def one_block(block_pair):
        block_index, query_block = block_pair
        scores = jnp.einsum(
            "qhd,khd->hqk", query_block, key_rows, preferred_element_type=jnp.float32
        )
        allowed = allowed_mask(
            block_index * block_rows, block_rows, row_total, seq_length, block_size
        )
        scores = jnp.where(allowed[None], scores, masked_score)
        top_score = jnp.max(scores, axis=-1, keepdims=True)
        exp_scores = jnp.exp(scores - top_score)
        exp_total = jnp.sum(exp_scores, axis=-1, keepdims=True)
        probabilities = (exp_scores / exp_total).astype(jnp.bfloat16)
        context = jnp.einsum(
            "hqk,khd->qhd", probabilities, value_rows, preferred_element_type=jnp.float32
        )
        return (context.astype(jnp.bfloat16), top_score[..., 0] + jnp.log(exp_total[..., 0]))

    contexts, log_sums = lax.map(
        one_block, (jnp.arange(block_count, dtype=jnp.int32), query_blocks)
    )
    return (contexts.reshape(row_total, local_heads * head_size), log_sums)


def attend_back(query_rows, key_rows, value_rows, context_grad, log_sums, seq_length, block_size):
    row_total, local_heads, head_size = query_rows.shape
    block_rows = min(512, row_total)
    block_count = row_total // block_rows
    query_blocks = query_rows.reshape(block_count, block_rows, local_heads, head_size)
    grad_blocks = context_grad.reshape(block_count, block_rows, local_heads, head_size)

    def one_block(running, block_pack):
        key_grad, value_grad = running
        block_index, query_block, grad_block, log_block = block_pack
        scores = jnp.einsum(
            "qhd,khd->hqk", query_block, key_rows, preferred_element_type=jnp.float32
        )
        allowed = allowed_mask(
            block_index * block_rows, block_rows, row_total, seq_length, block_size
        )
        probabilities = jnp.where(allowed[None], jnp.exp(scores - log_block[..., None]), 0.0)
        prob_grad = jnp.einsum(
            "qhd,khd->hqk", grad_block, value_rows, preferred_element_type=jnp.float32
        )
        row_dot = jnp.sum(prob_grad * probabilities, axis=-1, keepdims=True)
        score_grad = (probabilities * (prob_grad - row_dot)).astype(jnp.bfloat16)
        query_grad = jnp.einsum(
            "hqk,khd->qhd", score_grad, key_rows, preferred_element_type=jnp.float32
        )
        key_grad = key_grad + jnp.einsum(
            "hqk,qhd->khd", score_grad, query_block, preferred_element_type=jnp.float32
        )
        value_grad = value_grad + jnp.einsum(
            "hqk,qhd->khd",
            probabilities.astype(jnp.bfloat16),
            grad_block,
            preferred_element_type=jnp.float32,
        )
        return ((key_grad, value_grad), query_grad)

    empty = jnp.zeros((row_total, local_heads, head_size), jnp.float32)
    (key_grad, value_grad), query_grads = lax.scan(
        one_block,
        (empty, empty),
        (jnp.arange(block_count, dtype=jnp.int32), query_blocks, grad_blocks, log_sums),
    )
    width = local_heads * head_size
    return (
        query_grads.reshape(row_total, width),
        key_grad.reshape(row_total, width),
        value_grad.reshape(row_total, width),
    )


def on_device(
    tokens,
    seq_lens,
    block_sizes,
    w_query,
    b_query,
    w_key,
    w_value,
    b_value,
    w_out,
    b_out,
    gain_one,
    shift_one,
    w_up,
    b_up,
    w_down,
    b_down,
    gain_two,
    shift_two,
    cotangent,
):
    micro_total = seq_lens.shape[0]
    seq_rows = tokens.shape[0] // micro_total
    head_cols = w_query.shape[1]
    local_heads = head_cols // HEAD
    model_width = tokens.shape[1]
    own_cols = model_width // lax.axis_size("tensor")
    column_start = lax.axis_index("tensor") * own_cols
    query_bias = b_query.astype(jnp.float32)
    value_bias = b_value.astype(jnp.float32)
    up_bias = b_up.astype(jnp.float32)
    owned = (
        w_query,
        w_key,
        w_value,
        w_out,
        w_up,
        w_down,
        b_out,
        gain_one,
        shift_one,
        b_down,
        gain_two,
        shift_two,
    )

    def shaped(flat_rows):
        return flat_rows.reshape(seq_rows, local_heads, HEAD)

    layer_outputs = []
    input_grads = []
    totals = None
    for micro_index in range(micro_total):
        rows_in = tokens[micro_index * seq_rows : (micro_index + 1) * seq_rows]
        upstream = cotangent[micro_index * seq_rows : (micro_index + 1) * seq_rows].astype(
            jnp.float32
        )
        seq_length = seq_lens[micro_index]
        block_size = block_sizes[micro_index]
        forward_set = (
            lax.all_gather(owned[0], "dp", axis=0, tiled=True),
            lax.all_gather(owned[1], "dp", axis=0, tiled=True),
            lax.all_gather(owned[2], "dp", axis=0, tiled=True),
            lax.all_gather(owned[3], "dp", axis=1, tiled=True),
            lax.all_gather(owned[4], "dp", axis=0, tiled=True),
            lax.all_gather(owned[5], "dp", axis=1, tiled=True),
            lax.all_gather(owned[6], "dp", axis=0, tiled=True),
            lax.all_gather(owned[7], "dp", axis=0, tiled=True),
            lax.all_gather(owned[8], "dp", axis=0, tiled=True),
            lax.all_gather(owned[9], "dp", axis=0, tiled=True),
            lax.all_gather(owned[10], "dp", axis=0, tiled=True),
            lax.all_gather(owned[11], "dp", axis=0, tiled=True),
        )
        (
            full_query,
            full_key,
            full_value,
            full_out,
            full_up,
            full_down,
            full_out_bias,
            full_gain_one,
            full_shift_one,
            full_down_bias,
            full_gain_two,
            full_shift_two,
        ) = forward_set
        out_bias = full_out_bias.astype(jnp.float32)
        down_bias = full_down_bias.astype(jnp.float32)
        first_gain = full_gain_one.astype(jnp.float32)
        first_shift = full_shift_one.astype(jnp.float32)
        second_gain = full_gain_two.astype(jnp.float32)
        second_shift = full_shift_two.astype(jnp.float32)
        query_rows = ((matmul(rows_in, full_query) + query_bias) * 0.125).astype(jnp.bfloat16)
        key_rows = matmul(rows_in, full_key).astype(jnp.bfloat16)
        value_rows = (matmul(rows_in, full_value) + value_bias).astype(jnp.bfloat16)
        context, log_sums = attend(
            shaped(query_rows), shaped(key_rows), shaped(value_rows), seq_length, block_size
        )
        attended = lax.psum(matmul(context, full_out), "tensor") + out_bias
        first_norm, first_hat, first_scale = norm_forward(
            rows_in.astype(jnp.float32) + attended, first_gain, first_shift
        )
        normed = first_norm.astype(jnp.bfloat16)
        expanded = matmul(normed, full_up) + up_bias
        normal_cdf = 0.5 * (1.0 + lax.erf(expanded * inv_root_two))
        hidden = (expanded * normal_cdf).astype(jnp.bfloat16)
        lowered = lax.psum(matmul(hidden, full_down), "tensor") + down_bias
        second_norm, second_hat, second_scale = norm_forward(
            normed.astype(jnp.float32) + lowered, second_gain, second_shift
        )
        layer_outputs.append(second_norm.astype(jnp.bfloat16))
        second_grad, grad_gain_two, grad_shift_two = norm_backward(
            upstream, second_hat, second_scale, second_gain
        )
        down_bias_grad = jnp.sum(second_grad, axis=0)
        second_low = second_grad.astype(jnp.bfloat16)
        down_grad = contract_rows(hidden, second_low)
        hidden_grad = contract_cols(second_low, full_down)
        expanded_grad = hidden_grad * (
            normal_cdf + expanded * jnp.exp(-0.5 * expanded * expanded) * inv_root_tau
        )
        up_bias_grad = jnp.sum(expanded_grad, axis=0)
        expanded_low = expanded_grad.astype(jnp.bfloat16)
        up_grad = contract_rows(normed, expanded_low)
        normed_grad = lax.psum(contract_cols(expanded_low, full_up), "tensor") + second_grad
        first_grad, grad_gain_one, grad_shift_one = norm_backward(
            normed_grad, first_hat, first_scale, first_gain
        )
        out_bias_grad = jnp.sum(first_grad, axis=0)
        first_low = first_grad.astype(jnp.bfloat16)
        out_grad = contract_rows(context, first_low)
        context_grad = contract_cols(first_low, full_out).astype(jnp.bfloat16)
        query_grad, key_grad, value_grad = attend_back(
            shaped(query_rows),
            shaped(key_rows),
            shaped(value_rows),
            shaped(context_grad),
            log_sums,
            seq_length,
            block_size,
        )
        query_grad = query_grad * 0.125
        query_bias_grad = jnp.sum(query_grad, axis=0)
        value_bias_grad = jnp.sum(value_grad, axis=0)
        query_low = query_grad.astype(jnp.bfloat16)
        key_low = key_grad.astype(jnp.bfloat16)
        value_low = value_grad.astype(jnp.bfloat16)
        query_w_grad = contract_rows(rows_in, query_low)
        key_w_grad = contract_rows(rows_in, key_low)
        value_w_grad = contract_rows(rows_in, value_low)
        input_term = (
            contract_cols(query_low, full_query)
            + contract_cols(key_low, full_key)
            + contract_cols(value_low, full_value)
        )
        own_grad = lax.psum_scatter(
            input_term.astype(jnp.bfloat16), "tensor", scatter_dimension=1, tiled=True
        ).astype(jnp.float32)
        input_grads.append(
            own_grad + lax.dynamic_slice_in_dim(first_grad, column_start, own_cols, 1)
        )
        terms = (
            query_w_grad,
            query_bias_grad,
            key_w_grad,
            value_w_grad,
            value_bias_grad,
            out_grad,
            out_bias_grad,
            grad_gain_one,
            grad_shift_one,
            up_grad,
            up_bias_grad,
            down_grad,
            down_bias_grad,
            grad_gain_two,
            grad_shift_two,
        )
        if totals is None:
            totals = terms
        else:
            totals = tuple((running + addend for running, addend in zip(totals, terms)))
    summed = (
        lax.psum_scatter(totals[0], "dp", scatter_dimension=0, tiled=True),
        lax.psum_scatter(totals[2], "dp", scatter_dimension=0, tiled=True),
        lax.psum_scatter(totals[3], "dp", scatter_dimension=0, tiled=True),
        lax.psum_scatter(totals[5], "dp", scatter_dimension=1, tiled=True),
        lax.psum_scatter(totals[9], "dp", scatter_dimension=0, tiled=True),
        lax.psum_scatter(totals[11], "dp", scatter_dimension=1, tiled=True),
        lax.psum_scatter(totals[6], "dp", scatter_dimension=0, tiled=True),
        lax.psum_scatter(totals[7], "dp", scatter_dimension=0, tiled=True),
        lax.psum_scatter(totals[8], "dp", scatter_dimension=0, tiled=True),
        lax.psum_scatter(totals[12], "dp", scatter_dimension=0, tiled=True),
        lax.psum_scatter(totals[13], "dp", scatter_dimension=0, tiled=True),
        lax.psum_scatter(totals[14], "dp", scatter_dimension=0, tiled=True),
    )
    bias_sums = lax.psum((totals[1], totals[4], totals[10]), "dp")
    return (
        jnp.concatenate(layer_outputs, 0),
        jnp.concatenate(input_grads, 0),
        summed[0],
        bias_sums[0],
        summed[1],
        summed[2],
        bias_sums[1],
        summed[3],
        summed[6],
        summed[7],
        summed[8],
        summed[4],
        bias_sums[2],
        summed[5],
        summed[9],
        summed[10],
        summed[11],
    )


def solution(mesh):
    in_specs = (
        P("dp", None),
        P("dp"),
        P("dp"),
        P("dp", "tensor"),
        P("tensor"),
        P("dp", "tensor"),
        P("dp", "tensor"),
        P("tensor"),
        P("tensor", "dp"),
        P("dp"),
        P("dp"),
        P("dp"),
        P("dp", "tensor"),
        P("tensor"),
        P("tensor", "dp"),
        P("dp"),
        P("dp"),
        P("dp"),
        P("dp", None),
    )
    out_specs = (
        P("dp", None),
        P("dp", "tensor"),
        P("dp", "tensor"),
        P("tensor"),
        P("dp", "tensor"),
        P("dp", "tensor"),
        P("tensor"),
        P("tensor", "dp"),
        P("dp"),
        P("dp"),
        P("dp"),
        P("dp", "tensor"),
        P("tensor"),
        P("tensor", "dp"),
        P("dp"),
        P("dp"),
        P("dp"),
    )
    return jax.shard_map(
        on_device, mesh=mesh, in_specs=in_specs, out_specs=out_specs, check_vma=False
    )
```

profile of v0, /device:TPU:0, one launch (start us, length us, event | category | flops | bytes accessed | tf_op | source)
XLA Modules:
  0.0 1132.8 jit_solution(600460367562046693)
XLA Ops:
  8.1 33.1 %all_gather.48 = bf16[768,192]{1,0:T(8,128)(2,1)S(1)} all-gather(bf16[96,192]{1,0:T(8,128)(2,1)} %param.30), channel_id=1, replica_groups=mesh['dp'=8,'tensor'=4] {'dp'}, dimensions={0}, use_global_device_ids=true | all-gather | bytes 331776 | tf_op jit(solution)/shard_map/all_gather | solution.py:194
  46.2 31.1 %all_gather.50 = bf16[768,192]{1,0:T(8,128)(2,1)S(1)} all-gather(bf16[96,192]{1,0:T(8,128)(2,1)S(1)} %copy-done.68), channel_id=1, replica_groups=mesh['dp'=8,'tensor'=4] {'dp'}, dimensions={0}, use_global_device_ids=true | all-gather | bytes 331776 | tf_op jit(solution)/shard_map/all_gather | solution.py:196
  79.4 31.1 %all_gather.49 = bf16[768,192]{1,0:T(8,128)(2,1)S(1)} all-gather(bf16[96,192]{1,0:T(8,128)(2,1)S(1)} %copy-done.69), channel_id=1, replica_groups=mesh['dp'=8,'tensor'=4] {'dp'}, dimensions={0}, use_global_device_ids=true | all-gather | bytes 331776 | tf_op jit(solution)/shard_map/all_gather | solution.py:195
  114.2 21.0 %while.66 = (s32[]{:T(128)}, bf16[2,512,3,64]{1,3,2,0:T(8,128)(2,1)S(1)}, f32[2,3,512]{2,1,0:T(4,128)S(1)}, s32[]{:T(128)}, s32[]{:T(128)}, /*index=5*/s32[2]{0:...) while((s32[]{:T(128)}, ...), condition=%wide.region_3.4_spmd, body=%wide.region_0.3_spmd.sunk | while | flops 419015680 | bytes 22240444 | solution.py:78
  135.8 31.2 %all_gather.51 = bf16[192,768]{0,1:T(8,128)(2,1)S(1)} all-gather(bf16[192,96]{0,1:T(8,128)(2,1)S(1)} %copy.74), channel_id=1, replica_groups=mesh['dp'=8,'tensor'=4] {'dp'}, dimensions={1}, use_global_device_ids=true | all-gather | bytes 331776 | tf_op jit(solution)/shard_map/all_gather | solution.py:197
  168.0 21.0 %while.67 = (s32[]{:T(128)}, bf16[2,512,3,64]{1,3,2,0:T(8,128)(2,1)S(1)}, f32[2,3,512]{2,1,0:T(4,128)S(1)}, s32[]{:T(128)}, s32[]{:T(128)}, /*index=5*/s32[2]{0:...) while((s32[]{:T(128)}, ...), condition=%wide.region_13.14_spmd, body=%wide.region_10.13_spmd.sunk | while | flops 419015680 | bytes 22240444 | solution.py:78
  198.3 38.0 %all-reduce.16 = (bf16[768]{0:T(1024)(128)(2,1)S(1)}, bf16[768]{0:T(1024)(128)(2,1)S(1)}, bf16[768]{0:T(1024)(128)(2,1)S(1)}, bf16[768]{0:T(1024)(128)(2,1)S(1)}...) all-reduce(bf16[768]{0:T(1024)(128)(2,1)S(1)} %dynamic-update-slice, ...), channel_id=1, replica_groups=mesh['dp'=8,'tensor'=4] {'dp'}, use_global_device_ids=true, to_apply=%add | all-reduce | flops 4608 | bytes 18432
  236.4 78.9 %all-reduce.25.cloned.1.call-done = (f32[1024,768]{1,0:T(8,128)}, f32[1024,768]{1,0:T(8,128)}) async-done(((f32[1024,768]{1,0:T(8,128)}, f32[1024,768]{1,0:T(8,128)}), (f32[1024,768]{1,0:T(8,128)}, f32[1024,768]{1,0:T(8,128)})) %all-reduce.25.cloned.1.call-update) | async-done | bytes 6291472 | tf_op jit(solution)/shard_map/psum | solution.py:233
  315.4 4.7 fusion.169
  329.7 3.8 multiply_convert_fusion.3
  333.5 4.9 fusion.179
  342.1 119.6 %all-reduce.23.cloned.1.call-done = (f32[1024,768]{1,0:T(8,128)}, f32[1024,768]{1,0:T(8,128)}) async-done(((f32[1024,768]{1,0:T(8,128)}, f32[1024,768]{1,0:T(8,128)}), (f32[1024,768]{1,0:T(8,128)}, f32[1024,768]{1,0:T(8,128)})) %all-reduce.23.cloned.1.call-update) | async-done | bytes 6291472 | tf_op jit(solution)/shard_map/psum | solution.py:241
  461.7 4.2 fusion.167
  467.9 3.6 convert_reduce_fusion
  471.5 4.6 fusion.161
  489.7 119.9 %all-reduce.21.cloned.1.call-done = (f32[1024,768]{1,0:T(8,128)}, f32[1024,768]{1,0:T(8,128)}) async-done(((f32[1024,768]{1,0:T(8,128)}, f32[1024,768]{1,0:T(8,128)}), (f32[1024,768]{1,0:T(8,128)}, f32[1024,768]{1,0:T(8,128)})) %all-reduce.21.cloned.1.call-update) | async-done | bytes 6291472 | tf_op jit(solution)/shard_map/psum | solution.py:259
  609.6 5.4 multiply_reduce_fusion.3
  617.0 3.6 fusion.166
  628.8 44.0 %while.68 = (s32[]{:T(128)}, f32[1024,3,64]{0,2,1:T(8,128)}, f32[1024,3,64]{0,2,1:T(8,128)}, f32[2,512,3,64]{1,3,2,0:T(8,128)}, bf16[2,512,3,64]{1,3,2,0:T(8,128...) while((s32[]{:T(128)}, f32[1024,3,64]{0,2,1:T(8,128)}, ...), condition=%wide.region_27.28_spmd.clone, body=%wide.region_25.27_spmd.clone.sunk | while | flops 1028402176 | bytes 118828048 | solution.py:121
  636.0 3.6 multiply_reduce_fusion.16
  657.8 3.7 multiply_reduce_fusion.16
  669.1 3.7 fusion.327
  675.1 40.6 %while.69 = (s32[]{:T(128)}, f32[1024,3,64]{0,2,1:T(8,128)}, f32[1024,3,64]{0,2,1:T(8,128)}, f32[2,512,3,64]{1,3,2,0:T(8,128)}, bf16[2,512,3,64]{1,3,2,0:T(8,128...) while((s32[]{:T(128)}, f32[1024,3,64]{0,2,1:T(8,128)}, ...), condition=%wide.region_36.37_spmd.clone, body=%wide.region_34.36_spmd.clone.sunk | while | flops 1028402176 | bytes 114159056 | solution.py:121
  712.1 3.6 fusion.343
  743.9 4.0 fusion.143
  750.9 3.5 fusion.139
  761.0 37.7 %all-reduce.12 = (f32[192]{0:T(256)}, f32[192]{0:T(256)}, f32[768]{0:T(1024)S(1)}, f32[768]{0:T(1024)S(1)}, f32[768]{0:T(1024)S(1)}, /*index=5*/f32[768]{0:T(102...) all-reduce(f32[192]{0:T(256)S(1)} %add.515, ...), channel_id=1, replica_groups=mesh['dp'=8,'tensor'=4] {'dp'}, use_global_device_ids=true, to_apply=%region_41.42 | all-reduce | flops 5760 | bytes 46080 | tf_op jit(solution)/shard_map/psum | solution.py:331
  811.7 38.2 %reduce-scatter.33.cloned.1.call-done = f32[96,192]{1,0:T(8,128)} async-done(((f32[768,192]{1,0:T(8,128)}), f32[96,192]{1,0:T(8,128)}) %reduce-scatter.33.cloned.1.call-update) | async-done | bytes 73744
  850.0 65.4 %reduce-scatter.31.cloned.1.call-done = f32[96,192]{1,0:T(8,128)} async-done(((f32[768,192]{1,0:T(8,128)}), f32[96,192]{1,0:T(8,128)}) %reduce-scatter.31.cloned.1.call-update) | async-done | bytes 73744
  915.4 65.7 %reduce-scatter.29.cloned.1.call-done = f32[96,192]{1,0:T(8,128)} async-done(((f32[768,192]{1,0:T(8,128)}), f32[96,192]{1,0:T(8,128)}) %reduce-scatter.29.cloned.1.call-update) | async-done | bytes 73744
  981.1 72.0 %reduce-scatter.23.cloned.1.call-done = f32[768,96]{0,1:T(8,128)} async-done(((f32[768,768]{0,1:T(8,128)}), f32[768,96]{0,1:T(8,128)}) %reduce-scatter.23.cloned.1.call-update) | async-done | bytes 294928 | tf_op jit(solution)/shard_map/reduce_scatter | solution.py:323
  1053.1 72.1 %reduce-scatter.21.cloned.1.call-done = f32[96,768]{1,0:T(8,128)} async-done(((f32[768,768]{1,0:T(8,128)}), f32[96,768]{1,0:T(8,128)}) %reduce-scatter.21.cloned.1.call-update) | async-done | bytes 294928 | tf_op jit(solution)/shard_map/reduce_scatter | solution.py:322
  (513 shorter events, 215.6 us)
Async XLA Ops:
  8.0 36.7 %copy-start.23 = (bf16[2048,768]{1,0:T(8,128)(2,1)S(1)}, bf16[2048,768]{1,0:T(8,128)(2,1)}, u32[]{:S(2)}) copy-start(bf16[2048,768]{1,0:T(8,128)(2,1)} %param.27) | copy-start | bytes 9437188
  8.0 307.3 %all-reduce.25.cloned.1.call-start = ((), (), s32[]{:S(2)}) async-start(), calls=%async_computation.20 | async-start | bytes 12582912 | tf_op jit(solution)/shard_map/psum | solution.py:233
  41.9 35.4 %copy-start.93 = (bf16[192]{0:T(256)(128)(2,1)S(1)}, bf16[192]{0:T(256)(128)(2,1)}, u32[]{:S(2)}) copy-start(bf16[192]{0:T(256)(128)(2,1)} %param.34) | copy-start | bytes 1156
  46.2 33.2 %copy-start.69 = (bf16[96,192]{1,0:T(8,128)(2,1)S(1)}, bf16[96,192]{1,0:T(8,128)(2,1)}, u32[]{:S(2)}) copy-start(bf16[96,192]{1,0:T(8,128)(2,1)} %param.32) | copy-start | bytes 110596
  77.3 34.0 %copy-start.43 = (bf16[768,192]{1,0:T(8,128)(2,1)}, bf16[768,192]{1,0:T(8,128)(2,1)S(1)}, u32[]{:S(2)}) copy-start(bf16[768,192]{1,0:T(8,128)(2,1)S(1)} %all_gather.50) | copy-start | bytes 884740
  77.3 33.2 %copy-start.24 = (bf16[2048,768]{1,0:T(8,128)(2,1)S(1)}, bf16[2048,768]{1,0:T(8,128)(2,1)}, u32[]{:S(2)}) copy-start(bf16[2048,768]{1,0:T(8,128)(2,1)} %param.27) | copy-start | bytes 9437188
  79.4 32.5 %copy-start.64 = (bf16[1024,192]{0,1:T(8,128)(2,1)S(1)}, bf16[1024,192]{0,1:T(8,128)(2,1)}, u32[]{:S(2)}) copy-start(bf16[1024,192]{0,1:T(8,128)(2,1)} %fusion.122) | copy-start | bytes 1179652
  114.2 21.5 %copy-start.70 = (bf16[192,96]{1,0:T(8,128)(2,1)S(1)}, bf16[192,96]{1,0:T(8,128)(2,1)}, u32[]{:S(2)}) copy-start(bf16[192,96]{1,0:T(8,128)(2,1)} %param.35) | copy-start | bytes 110596
  114.2 52.8 %copy-start.63 = (bf16[1024,192]{0,1:T(8,128)(2,1)S(1)}, bf16[1024,192]{0,1:T(8,128)(2,1)}, u32[]{:S(2)}) copy-start(bf16[1024,192]{0,1:T(8,128)(2,1)} %fusion.123) | copy-start | bytes 1179652
  135.7 54.0 %copy-start.57 = (bf16[24,8,2,512]{3,1,2,0:T(8,128)(2,1)}, bf16[24,8,2,512]{3,1,2,0:T(8,128)(2,1)S(1)}, u32[]{:S(2)}) copy-start(bf16[24,8,2,512]{3,1,2,0:T(8,128)(2,1)S(1)} %copy.101) | copy-start | bytes 1179652
  194.4 42.0 %copy-start.85 = (bf16[768]{0:T(1024)(128)(2,1)S(1)}, bf16[768]{0:T(1024)(128)(2,1)}, u32[]{:S(2)}) copy-start(bf16[768]{0:T(1024)(128)(2,1)} %param.40) | copy-start | bytes 4612
  194.4 130.3 %all-gather.3.cloned.1.call-start = ((), (), s32[]{:S(2)}) async-start(), calls=%async_computation.8 | async-start | bytes 1327104 | tf_op jit(solution)/shard_map/all_gather | solution.py:198
  195.0 138.5 %all-gather.5.cloned.1.call-start = ((), (), s32[]{:S(2)}) async-start(), calls=%async_computation.9 | async-start | bytes 1327104 | tf_op jit(solution)/shard_map/all_gather | solution.py:199
  195.6 266.2 %all-reduce.23.cloned.1.call-start = ((), (), s32[]{:S(2)}) async-start(), calls=%async_computation.19 | async-start | bytes 12582912 | tf_op jit(solution)/shard_map/psum | solution.py:241
  324.7 137.1 %copy-start.40 = (bf16[1024,768]{1,0:T(8,128)(2,1)}, bf16[1024,768]{1,0:T(8,128)(2,1)S(1)}, u32[]{:S(2)}) copy-start(bf16[1024,768]{1,0:T(8,128)(2,1)S(1)} %get-tuple-element.1173) | copy-start | bytes 4718596
  341.6 268.0 %all-reduce.21.cloned.1.call-start = ((), (), s32[]{:S(2)}) async-start(), calls=%async_computation.18 | async-start | bytes 12582912 | tf_op jit(solution)/shard_map/psum | solution.py:259
  479.0 7.3 copy-start.103
  489.4 312.8 %reduce-scatter.35.cloned.1.call-start = ((), (), s32[]{:S(2)}) async-start(), calls=%async_computation.17 | async-start | bytes 884736
  609.6 7.4 copy-start.59
  627.4 176.5 %reduce-scatter.25.cloned.1.call-start = ((), (), s32[]{:S(2)}) async-start(), calls=%async_computation.12 | async-start | bytes 1966080
  628.8 46.3 %copy-start.9 = (bf16[1024,3,64]{0,2,1:T(8,128)(2,1)S(1)}, bf16[1024,3,64]{0,2,1:T(8,128)(2,1)}, u32[]{:S(2)}) copy-start(bf16[1024,3,64]{0,2,1:T(8,128)(2,1)} %copy-done.8) | copy-start | bytes 1179652
  628.8 7.2 copy-start.28
  650.4 6.6 copy-start.10
  650.5 7.3 copy-start.28
  675.3 7.7 copy-start.26
  695.3 7.7 copy-start.26
  724.0 81.1 %reduce-scatter.27.cloned.1.call-start = ((), (), s32[]{:S(2)}) async-start(), calls=%async_computation.13 | async-start | bytes 1966080
  727.8 122.2 %reduce-scatter.33.cloned.1.call-start = ((), (), s32[]{:S(2)}) async-start(), calls=%async_computation.16 | async-start | bytes 884736
  733.6 181.8 %reduce-scatter.31.cloned.1.call-start = ((), (), s32[]{:S(2)}) async-start(), calls=%async_computation.15 | async-start | bytes 884736
  738.7 242.4 %reduce-scatter.29.cloned.1.call-start = ((), (), s32[]{:S(2)}) async-start(), calls=%async_computation.14 | async-start | bytes 884736
  743.8 309.3 %reduce-scatter.23.cloned.1.call-start = ((), (), s32[]{:S(2)}) async-start(), calls=%async_computation.11 | async-start | bytes 2654208 | tf_op jit(solution)/shard_map/reduce_scatter | solution.py:323
  750.9 374.4 %reduce-scatter.21.cloned.1.call-start = ((), (), s32[]{:S(2)}) async-start(), calls=%async_computation.10 | async-start | bytes 2654208 | tf_op jit(solution)/shard_map/reduce_scatter | solution.py:322
  (107 other events, 360.2 us)
Sparse Core Ops, SparseCore 0:
  194.5 120.7 all-reduce.24
  341.7 119.9 all-reduce.22
  489.6 119.9 all-reduce.20
Sparse Core Ops, SparseCore 1:
  197.1 42.1 all-gather.2
  241.3 40.2 all-gather.4
  627.5 62.7 reduce-scatter.34
  724.1 28.2 reduce-scatter.24
  755.0 28.1 reduce-scatter.26
  787.4 62.6 reduce-scatter.32
  853.7 61.6 reduce-scatter.30
  919.5 61.5 reduce-scatter.28
  985.0 68.0 reduce-scatter.22
  1057.2 68.0 reduce-scatter.20
where the time goes:
time: 1140 us; the launch traced here: 1130 us
  waiting for transfers between devices  633 us (56%)
  blocking collectives  202 us (18%)
  matrix products  137 us (12%)
  other arithmetic  89.8 us (8%)
  local copies, waits for them, and re-layouts  43.1 us (4%)
  between operations  19.9 us (2%)
    unnamed x19, waiting for transfers between devices  171 us
    psum x1, waiting for transfers between devices, on_device(): lax.psum(contract_cols(expanded_low, full_up), 'tensor') + second_grad  120 us
    psum x1, waiting for transfers between devices, on_device(): lowered = lax.psum(matmul(hidden, full_down), 'tensor') + down_bias  120 us
    psum x1, waiting for transfers between devices, on_device(): attended = lax.psum(matmul(context, full_out), 'tensor') + out_bias  78.9 us
    reduce_scatter x1, waiting for transfers between devices, on_device(): lax.psum_scatter(totals[9], 'dp', scatter_dimension=0, tiled=True)  72.1 us
    reduce_scatter x1, waiting for transfers between devices, on_device(): lax.psum_scatter(totals[11], 'dp', scatter_dimension=1, tiled=True)  72 us
    unnamed x1, blocking collectives  38 us
    psum x1, blocking collectives, on_device(): bias_sums = lax.psum((totals[1], totals[4], totals[10]), 'dp')  37.7 us
  transfers between devices with their start and end apart: 13, of which 8 were waited for; matrix products, arithmetic and copies ran while one was open for 14% of the time, Pallas kernels for 0%

commit v1 on v0

--- a/solution.py
+++ b/solution.py
@@ -8,6 +8,11 @@
 inv_root_two = 0.7071067811865476
 inv_root_tau = 0.3989422804014327
 masked_score = -1000000000.0
+
+
+def add_all(shard, mesh_axis):
+    shards = lax.all_gather(shard, mesh_axis)
+    return jnp.sum(shards, axis=0)
 
 
 def matmul(first_operand, second_operand):
@@ -230,7 +235,7 @@
         context, log_sums = attend(
             shaped(query_rows), shaped(key_rows), shaped(value_rows), seq_length, block_size
         )
-        attended = lax.psum(matmul(context, full_out), "tensor") + out_bias
+        attended = add_all(matmul(context, full_out), "tensor") + out_bias
         first_norm, first_hat, first_scale = norm_forward(
             rows_in.astype(jnp.float32) + attended, first_gain, first_shift
         )

time: 1140 us -> 1220 us (1.070)
  waiting for transfers between devices: 633 us -> 694 us
  other arithmetic: 89.8 us -> 110 us
    all_gather x0 -> x2, waiting for transfers between devices: none -> 84.5 us  [add_all(): shards = lax.all_gather(shard, mesh_axis)]
    psum x1 -> x0, waiting for transfers between devices: 78.9 us -> none  [on_device(): attended = lax.psum(matmul(context, full_out), 'tensor') + out_bias]
    all_gather x1, waiting for transfers between devices: 0.01 us -> 33 us  [on_device(): lax.all_gather(owned[5], 'dp', axis=1, tiled=True)]
    all_gather x1, waiting for transfers between devices: 0.01 us -> 27.1 us  [on_device(): lax.all_gather(owned[4], 'dp', axis=0, tiled=True)]
    reduce_sum x0 -> x2, other arithmetic: none -> 14.9 us  [add_all(): return jnp.sum(shards, axis=0)]
    unnamed x214 -> x222, local copies, waits for them, and re-layouts: 28.8 us -> 26.9 us
    unnamed x19 -> x20, waiting for transfers between devices: 171 us -> 171 us
  transfers between devices with their start and end apart: 13 -> 14, of which waited for: 8 -> 11; matrix products, arithmetic and copies ran while one was open for 14% -> 17% of each run, Pallas kernels for 0% -> 0%
where the time goes in v1:
time: 1220 us; the launch traced here: 1210 us
  waiting for transfers between devices  694 us (57%)
  blocking collectives  201 us (16%)
  matrix products  141 us (12%)
  other arithmetic  110 us (9%)
  local copies, waits for them, and re-layouts  41 us (3%)
  between operations  18.6 us (2%)
    unnamed x20, waiting for transfers between devices  171 us
    psum x1, waiting for transfers between devices, on_device(): lax.psum(contract_cols(expanded_low, full_up), 'tensor') + second_grad  120 us
    psum x1, waiting for transfers between devices, on_device(): lowered = lax.psum(matmul(hidden, full_down), 'tensor') + down_bias  114 us
    all_gather x2, waiting for transfers between devices, add_all(): shards = lax.all_gather(shard, mesh_axis)  84.5 us
    reduce_scatter x1, waiting for transfers between devices, on_device(): lax.psum_scatter(totals[9], 'dp', scatter_dimension=0, tiled=True)  72 us
    reduce_scatter x1, waiting for transfers between devices, on_device(): lax.psum_scatter(totals[11], 'dp', scatter_dimension=1, tiled=True)  72 us
    psum x1, blocking collectives, on_device(): bias_sums = lax.psum((totals[1], totals[4], totals[10]), 'dp')  37.7 us
    unnamed x1, blocking collectives  37.5 us
  transfers between devices with their start and end apart: 14, of which 11 were waited for; matrix products, arithmetic and copies ran while one was open for 17% of the time, Pallas kernels for 0%

profile of v1, /device:TPU:0, one launch (start us, length us, event | category | flops | bytes accessed | tf_op | source)
XLA Modules:
  0.0 1213.2 jit_solution(17310380581113226937)
XLA Ops:
  7.3 33.0 %all_gather.60 = bf16[768,192]{1,0:T(8,128)(2,1)S(1)} all-gather(bf16[96,192]{1,0:T(8,128)(2,1)} %param.30), channel_id=1, replica_groups=mesh['dp'=8,'tensor'=4] {'dp'}, dimensions={0}, use_global_device_ids=true | all-gather | bytes 331776 | tf_op jit(solution)/shard_map/all_gather | solution.py:199
  43.3 31.1 %all_gather.62 = bf16[768,192]{1,0:T(8,128)(2,1)S(1)} all-gather(bf16[96,192]{1,0:T(8,128)(2,1)S(1)} %copy-done.65), channel_id=1, replica_groups=mesh['dp'=8,'tensor'=4] {'dp'}, dimensions={0}, use_global_device_ids=true | all-gather | bytes 331776 | tf_op jit(solution)/shard_map/all_gather | solution.py:201
  74.4 31.0 %all_gather.61 = bf16[768,192]{1,0:T(8,128)(2,1)S(1)} all-gather(bf16[96,192]{1,0:T(8,128)(2,1)S(1)} %copy-done.66), channel_id=1, replica_groups=mesh['dp'=8,'tensor'=4] {'dp'}, dimensions={0}, use_global_device_ids=true | all-gather | bytes 331776 | tf_op jit(solution)/shard_map/all_gather | solution.py:200
  111.6 21.0 %while.66 = (s32[]{:T(128)}, bf16[2,512,3,64]{1,3,2,0:T(8,128)(2,1)S(1)}, f32[2,3,512]{2,1,0:T(4,128)S(1)}, s32[]{:T(128)}, s32[]{:T(128)}, /*index=5*/s32[2]{0:...) while((s32[]{:T(128)}, ...), condition=%wide.region_3.4_spmd, body=%wide.region_0.3_spmd.sunk | while | flops 419015680 | bytes 22240444 | solution.py:83
  133.2 31.0 %all_gather.63 = bf16[192,768]{0,1:T(8,128)(2,1)S(1)} all-gather(bf16[192,96]{0,1:T(8,128)(2,1)S(1)} %copy.74), channel_id=1, replica_groups=mesh['dp'=8,'tensor'=4] {'dp'}, dimensions={1}, use_global_device_ids=true | all-gather | bytes 331776 | tf_op jit(solution)/shard_map/all_gather | solution.py:202
  174.2 21.0 %while.67 = (s32[]{:T(128)}, bf16[2,512,3,64]{1,3,2,0:T(8,128)(2,1)S(1)}, f32[2,3,512]{2,1,0:T(4,128)S(1)}, s32[]{:T(128)}, s32[]{:T(128)}, /*index=5*/s32[2]{0:...) while((s32[]{:T(128)}, ...), condition=%wide.region_13.14_spmd, body=%wide.region_10.13_spmd.sunk | while | flops 419015680 | bytes 22240444 | solution.py:83
  202.8 37.5 %all-reduce.15 = (bf16[768]{0:T(1024)(128)(2,1)S(1)}, bf16[768]{0:T(1024)(128)(2,1)S(1)}, bf16[768]{0:T(1024)(128)(2,1)S(1)}, bf16[768]{0:T(1024)(128)(2,1)}, bf...) all-reduce(bf16[768]{0:T(1024)(128)(2,1)S(1)} %dynamic-update-slice, ...), channel_id=1, replica_groups=mesh['dp'=8,'tensor'=4] {'dp'}, use_global_device_ids=true, to_apply=%add | all-reduce | flops 4608 | bytes 18432
  241.5 8.3 all-gather.11.cloned.1.call-done
  249.8 7.5 reduce_sum.376
  257.3 76.2 %all-gather.13.cloned.1.call-done = f32[4096,768]{1,0:T(8,128)} async-done(((f32[1024,768]{1,0:T(8,128)}), f32[4096,768]{1,0:T(8,128)}) %all-gather.13.cloned.1.call-update) | async-done | bytes 12582928 | tf_op jit(solution)/shard_map/all_gather | solution.py:14
  333.5 7.4 reduce_sum.381
  340.9 4.8 fusion.169
  349.7 27.1 %all-gather.7.cloned.1.call-done = bf16[768,768]{1,0:T(8,128)(2,1)} async-done(((bf16[96,768]{1,0:T(8,128)(2,1)}), bf16[768,768]{1,0:T(8,128)(2,1)}) %all-gather.7.cloned.1.call-update) | async-done | bytes 1179664 | tf_op jit(solution)/shard_map/all_gather | solution.py:203
  381.7 3.9 multiply_convert_fusion.3
  385.6 33.0 %all-gather.9.cloned.1.call-done = bf16[768,768]{0,1:T(8,128)(2,1)} async-done(((bf16[768,96]{0,1:T(8,128)(2,1)}), bf16[768,768]{0,1:T(8,128)(2,1)}) %all-gather.9.cloned.1.call-update) | async-done | bytes 1179664 | tf_op jit(solution)/shard_map/all_gather | solution.py:204
  418.7 5.0 fusion.179
  431.2 114.4 %all-reduce.21.cloned.1.call-done = (f32[1024,768]{1,0:T(8,128)}, f32[1024,768]{1,0:T(8,128)}) async-done(((f32[1024,768]{1,0:T(8,128)}, f32[1024,768]{1,0:T(8,128)}), (f32[1024,768]{1,0:T(8,128)}, f32[1024,768]{1,0:T(8,128)})) %all-reduce.21.cloned.1.call-update) | async-done | bytes 6291472 | tf_op jit(solution)/shard_map/psum | solution.py:246
  545.5 4.6 fusion.167
  555.8 4.6 fusion.161
  574.0 119.9 %all-reduce.19.cloned.1.call-done = (f32[1024,768]{1,0:T(8,128)}, f32[1024,768]{1,0:T(8,128)}) async-done(((f32[1024,768]{1,0:T(8,128)}, f32[1024,768]{1,0:T(8,128)}), (f32[1024,768]{1,0:T(8,128)}, f32[1024,768]{1,0:T(8,128)})) %all-reduce.19.cloned.1.call-update) | async-done | bytes 6291472 | tf_op jit(solution)/shard_map/psum | solution.py:264
  693.9 5.4 multiply_reduce_fusion.3
  712.5 41.3 %while.68 = (s32[]{:T(128)}, f32[1024,3,64]{0,2,1:T(8,128)}, f32[1024,3,64]{0,2,1:T(8,128)}, f32[2,512,3,64]{1,3,2,0:T(8,128)}, bf16[2,512,3,64]{1,3,2,0:T(8,128...) while((s32[]{:T(128)}, f32[1024,3,64]{0,2,1:T(8,128)}, ...), condition=%wide.region_27.28_spmd.clone, body=%wide.region_25.27_spmd.clone.sunk | while | flops 1028402176 | bytes 114109880 | solution.py:126
  750.2 3.7 fusion.327
  756.2 40.8 %while.69 = (s32[]{:T(128)}, f32[1024,3,64]{0,2,1:T(8,128)}, f32[1024,3,64]{0,2,1:T(8,128)}, f32[2,512,3,64]{1,3,2,0:T(8,128)}, bf16[2,512,3,64]{1,3,2,0:T(8,128...) while((s32[]{:T(128)}, f32[1024,3,64]{0,2,1:T(8,128)}, ...), condition=%wide.region_36.37_spmd.clone, body=%wide.region_34.36_spmd.clone.sunk | while | flops 1028402176 | bytes 115731952 | solution.py:126
  793.3 3.6 fusion.343
  825.1 4.0 fusion.143
  842.3 37.7 %all-reduce.12 = (f32[192]{0:T(256)}, f32[192]{0:T(256)}, f32[768]{0:T(1024)S(1)}, f32[768]{0:T(1024)S(1)}, f32[768]{0:T(1024)S(1)}, /*index=5*/f32[768]{0:T(102...) all-reduce(f32[192]{0:T(256)S(1)} %add.511, ...), channel_id=1, replica_groups=mesh['dp'=8,'tensor'=4] {'dp'}, use_global_device_ids=true, to_apply=%region_41.42 | all-reduce | flops 5760 | bytes 46080 | tf_op jit(solution)/shard_map/psum | solution.py:336
  892.9 38.2 %reduce-scatter.33.cloned.1.call-done = f32[96,192]{1,0:T(8,128)} async-done(((f32[768,192]{1,0:T(8,128)}), f32[96,192]{1,0:T(8,128)}) %reduce-scatter.33.cloned.1.call-update) | async-done | bytes 73744
  931.2 65.4 %reduce-scatter.31.cloned.1.call-done = f32[96,192]{1,0:T(8,128)} async-done(((f32[768,192]{1,0:T(8,128)}), f32[96,192]{1,0:T(8,128)}) %reduce-scatter.31.cloned.1.call-update) | async-done | bytes 73744
  996.6 65.6 %reduce-scatter.29.cloned.1.call-done = f32[96,192]{1,0:T(8,128)} async-done(((f32[768,192]{1,0:T(8,128)}), f32[96,192]{1,0:T(8,128)}) %reduce-scatter.29.cloned.1.call-update) | async-done | bytes 73744
  1062.2 72.0 %reduce-scatter.23.cloned.1.call-done = f32[768,96]{0,1:T(8,128)} async-done(((f32[768,768]{0,1:T(8,128)}), f32[768,96]{0,1:T(8,128)}) %reduce-scatter.23.cloned.1.call-update) | async-done | bytes 294928 | tf_op jit(solution)/shard_map/reduce_scatter | solution.py:328
  1134.2 72.0 %reduce-scatter.21.cloned.1.call-done = f32[96,768]{1,0:T(8,128)} async-done(((f32[768,768]{1,0:T(8,128)}), f32[96,768]{1,0:T(8,128)}) %reduce-scatter.21.cloned.1.call-update) | async-done | bytes 294928 | tf_op jit(solution)/shard_map/reduce_scatter | solution.py:327
  (518 shorter events, 240.9 us)
Async XLA Ops:
  7.2 36.1 %copy-start.65 = (bf16[96,192]{1,0:T(8,128)(2,1)S(1)}, bf16[96,192]{1,0:T(8,128)(2,1)}, u32[]{:S(2)}) copy-start(bf16[96,192]{1,0:T(8,128)(2,1)} %param.33) | copy-start | bytes 110596
  7.2 67.2 %copy-start.95 = (bf16[192]{0:T(256)(128)(2,1)S(1)}, bf16[192]{0:T(256)(128)(2,1)}, u32[]{:S(2)}) copy-start(bf16[192]{0:T(256)(128)(2,1)} %param.34) | copy-start | bytes 1156
  7.2 67.2 %copy-start.66 = (bf16[96,192]{1,0:T(8,128)(2,1)S(1)}, bf16[96,192]{1,0:T(8,128)(2,1)}, u32[]{:S(2)}) copy-start(bf16[96,192]{1,0:T(8,128)(2,1)} %param.32) | copy-start | bytes 110596
  7.2 242.6 %all-gather.11.cloned.1.call-start = ((), (), s32[]{:S(2)}) async-start(), calls=%async_computation.12 | async-start | bytes 15728640 | tf_op jit(solution)/shard_map/all_gather | solution.py:14
  40.2 126.6 %copy-start.49 = (bf16[768,192]{1,0:T(8,128)(2,1)}, bf16[768,192]{1,0:T(8,128)(2,1)S(1)}, u32[]{:S(2)}) copy-start(bf16[768,192]{1,0:T(8,128)(2,1)S(1)} %all_gather.60) | copy-start | bytes 884740
  43.0 64.6 %copy-start.89 = (s32[2]{0:T(128)S(1)}, s32[2]{0:T(128)}, u32[]{:S(2)}) copy-start(s32[2]{0:T(128)} %param.29) | copy-start | bytes 28
  43.0 65.9 %copy-start.90 = (s32[2]{0:T(128)S(1)}, s32[2]{0:T(128)}, u32[]{:S(2)}) copy-start(s32[2]{0:T(128)} %param.28) | copy-start | bytes 28
  74.4 97.6 %copy-start.39 = (bf16[768,192]{1,0:T(8,128)(2,1)}, bf16[768,192]{1,0:T(8,128)(2,1)S(1)}, u32[]{:S(2)}) copy-start(bf16[768,192]{1,0:T(8,128)(2,1)S(1)} %all_gather.62) | copy-start | bytes 884740
  105.4 64.6 %copy-start.51 = (bf16[768,192]{1,0:T(8,128)(2,1)}, bf16[768,192]{1,0:T(8,128)(2,1)S(1)}, u32[]{:S(2)}) copy-start(bf16[768,192]{1,0:T(8,128)(2,1)S(1)} %all_gather.61) | copy-start | bytes 884740
  111.6 21.5 %copy-start.67 = (bf16[192,96]{1,0:T(8,128)(2,1)S(1)}, bf16[192,96]{1,0:T(8,128)(2,1)}, u32[]{:S(2)}) copy-start(bf16[192,96]{1,0:T(8,128)(2,1)} %param.35) | copy-start | bytes 110596
  132.6 33.9 %copy-start.8 = (bf16[1024,3,64]{0,2,1:T(8,128)(2,1)}, bf16[1024,3,64]{0,2,1:T(8,128)(2,1)S(1)}, u32[]{:S(2)}) copy-start(bf16[1024,3,64]{0,2,1:T(8,128)(2,1)S(1)} %get-tuple-element.1732) | copy-start | bytes 1179652
  132.6 33.9 %copy-start.18 = (bf16[2,512,3,64]{1,3,2,0:T(8,128)(2,1)}, bf16[2,512,3,64]{1,3,2,0:T(8,128)(2,1)S(1)}, u32[]{:S(2)}) copy-start(bf16[2,512,3,64]{1,3,2,0:T(8,128)(2,1)S(1)} %get-tuple-element.1734) | copy-start | bytes 1179652
  132.6 33.9 %copy-start.32 = (bf16[1024,3,64]{0,2,1:T(8,128)(2,1)}, bf16[1024,3,64]{0,2,1:T(8,128)(2,1)S(1)}, u32[]{:S(2)}) copy-start(bf16[1024,3,64]{0,2,1:T(8,128)(2,1)S(1)} %get-tuple-element.1743) | copy-start | bytes 1179652
  132.6 33.9 %copy-start.60 = (f32[2,3,512]{2,1,0:T(4,128)}, f32[2,3,512]{2,1,0:T(4,128)S(1)}, u32[]{:S(2)}) copy-start(f32[2,3,512]{2,1,0:T(4,128)S(1)} %get-tuple-element.1674) | copy-start | bytes 36868
  133.1 33.4 %copy-start.53 = (bf16[24,8,2,512]{3,1,2,0:T(8,128)(2,1)}, bf16[24,8,2,512]{3,1,2,0:T(8,128)(2,1)S(1)}, u32[]{:S(2)}) copy-start(bf16[24,8,2,512]{3,1,2,0:T(8,128)(2,1)S(1)} %copy.101) | copy-start | bytes 1179652
  166.6 166.9 %all-gather.13.cloned.1.call-start = ((), (), s32[]{:S(2)}) async-start(), calls=%async_computation.13 | async-start | bytes 15728640 | tf_op jit(solution)/shard_map/all_gather | solution.py:14
  196.4 44.5 %copy-start.87 = (bf16[768]{0:T(1024)(128)(2,1)S(1)}, bf16[768]{0:T(1024)(128)(2,1)}, u32[]{:S(2)}) copy-start(bf16[768]{0:T(1024)(128)(2,1)} %param.40) | copy-start | bytes 4612
  198.8 178.0 %all-gather.7.cloned.1.call-start = ((), (), s32[]{:S(2)}) async-start(), calls=%async_computation.8 | async-start | bytes 1327104 | tf_op jit(solution)/shard_map/all_gather | solution.py:203
  199.5 219.2 %all-gather.9.cloned.1.call-start = ((), (), s32[]{:S(2)}) async-start(), calls=%async_computation.9 | async-start | bytes 1327104 | tf_op jit(solution)/shard_map/all_gather | solution.py:204
  200.1 345.5 %all-reduce.21.cloned.1.call-start = ((), (), s32[]{:S(2)}) async-start(), calls=%async_computation.21 | async-start | bytes 12582912 | tf_op jit(solution)/shard_map/psum | solution.py:246
  426.8 267.1 %all-reduce.19.cloned.1.call-start = ((), (), s32[]{:S(2)}) async-start(), calls=%async_computation.20 | async-start | bytes 12582912 | tf_op jit(solution)/shard_map/psum | solution.py:264
  573.8 309.7 %reduce-scatter.35.cloned.1.call-start = ((), (), s32[]{:S(2)}) async-start(), calls=%async_computation.19 | async-start | bytes 884736
  711.1 174.0 %reduce-scatter.25.cloned.1.call-start = ((), (), s32[]{:S(2)}) async-start(), calls=%async_computation.14 | async-start | bytes 1966080
  712.5 8.4 copy-start.23
  732.9 8.4 copy-start.23
  756.4 7.9 copy-start.21
  805.3 81.1 %reduce-scatter.27.cloned.1.call-start = ((), (), s32[]{:S(2)}) async-start(), calls=%async_computation.15 | async-start | bytes 1966080
  809.0 122.1 %reduce-scatter.33.cloned.1.call-start = ((), (), s32[]{:S(2)}) async-start(), calls=%async_computation.18 | async-start | bytes 884736
  814.8 181.8 %reduce-scatter.31.cloned.1.call-start = ((), (), s32[]{:S(2)}) async-start(), calls=%async_computation.17 | async-start | bytes 884736
  820.0 242.2 %reduce-scatter.29.cloned.1.call-start = ((), (), s32[]{:S(2)}) async-start(), calls=%async_computation.16 | async-start | bytes 884736
  825.1 309.1 %reduce-scatter.23.cloned.1.call-start = ((), (), s32[]{:S(2)}) async-start(), calls=%async_computation.11 | async-start | bytes 2654208 | tf_op jit(solution)/shard_map/reduce_scatter | solution.py:328
  832.1 374.1 %reduce-scatter.21.cloned.1.call-start = ((), (), s32[]{:S(2)}) async-start(), calls=%async_computation.10 | async-start | bytes 2654208 | tf_op jit(solution)/shard_map/reduce_scatter | solution.py:327
  (108 other events, 368.3 us)
Sparse Core Ops, SparseCore 0:
  166.6 83.1 all-gather.10
  251.4 82.0 all-gather.12
  335.7 41.0 all-gather.6
  378.8 39.8 all-gather.8
  426.9 118.5 all-reduce.20
  573.9 119.9 all-reduce.18
  711.3 62.7 reduce-scatter.34
  805.4 28.3 reduce-scatter.24
  836.3 28.1 reduce-scatter.26
  868.6 62.4 reduce-scatter.32
  935.0 61.5 reduce-scatter.30
  1000.7 61.4 reduce-scatter.28
  1066.3 67.8 reduce-scatter.22
  1138.1 68.0 reduce-scatter.20
